TPU v7x, 32 devices: a whole 2x2x4 slice. The times are simulated.
32 devices in a mesh: dp: 16 (over z, x, core), expert: 2 (over y).
Axes of the slice: x: 2, y: 2, z: 4, core: 2. Of those that a mesh axis runs over, the one named last changes fastest.
Arguments:
- hidden: bfloat16 [1024, 8192], P(('dp', 'expert')), may hold values from -6 to 6
- out_grad: bfloat16 [1024, 6144], P(('dp', 'expert')), may hold values from -6 to 6
- counts: int32 [32, 2], P(('dp', 'expert')), may hold values from 0 to 20, as said below
- route_index: int32 [32, 32], P(('dp', 'expert')), may hold values from 0 to 31, each once within a row
- keep: int32 [16], replicated, may hold values 0 or 1
Outputs:
- grad_blocks: float32 [2, 16, 2048, 1536], P('expert', 'dp')
- block_scales: float32 [2, 16, 2048, 12], P('expert', 'dp')
Inputs may be any that keep to these rules, and one draw needn't show every extreme that they name: Each row of counts sums to 32; for every index of dp, one expert receives exactly 20 rows from each of the 2 devices of that index.
All inputs are finite; a program needn't handle non-finite values. Where the computation divides by a largest or mean magnitude, that divisor is 1e-20 or more.
Results may differ from a plain program's by a relative error of at most 0.0003.
Values may be sent and summed in bfloat16 or wider, within the bound.
A program may use at most 128 MiB of HBM per device.

v0:
```python
import math

import jax
import jax.numpy as jnp
from jax import lax
from jax.sharding import PartitionSpec as P


def swapped(block, axis, bit):
    count = lax.axis_size(axis)
    route = []
    for low in range(count):
        high = low | 1 << bit
        if high != low and high < count:
            route += [(low, high), (high, low)]
    return lax.ppermute(block, axis, route)


def build_slots(rows_dev, counts_dev, perm_dev, capacity):
    offsets = jnp.cumsum(counts_dev) - counts_dev
    slots = jnp.arange(capacity, dtype=jnp.int32)
    position = offsets[:, None] + slots[None, :]
    position = jnp.minimum(position, rows_dev.shape[0] - 1)
    live = slots[None, :] < counts_dev[:, None]
    local = perm_dev[position]
    picked = rows_dev[local]
    return jnp.where(live[:, :, None], picked, jnp.zeros_like(picked))


def join_pair(mine, partner, replica, bit):
    lower = replica >> bit & 1 == 0
    first = jnp.concatenate([mine, partner], axis=1)
    second = jnp.concatenate([partner, mine], axis=1)
    return jnp.where(lower, first, second)


def on_device(hidden, out_grad, counts, route_index, keep):
    experts = lax.axis_size("expert")
    replicas = lax.axis_size("dp")
    side = math.isqrt(replicas)
    levels = side.bit_length() - 1
    tok_rows = hidden.shape[0]
    hidden_units = hidden.shape[1]
    width = out_grad.shape[1]
    capacity = max(tok_rows // 4, tok_rows // experts + 4)
    replica = lax.axis_index("dp")
    keep_here = keep[replica]
    grad_rows = jnp.where(keep_here > 0, out_grad, jnp.zeros_like(out_grad))
    send_h = build_slots(hidden, counts[0], route_index[0], capacity)
    send_g = build_slots(grad_rows, counts[0], route_index[0], capacity)
    recv_h, recv_g = (
        lax.all_to_all(send_h, "expert", split_axis=0, concat_axis=0, tiled=True),
        lax.all_to_all(send_g, "expert", split_axis=0, concat_axis=0, tiled=True),
    )
    slot_count = experts * capacity
    flat_h = recv_h.reshape(slot_count, hidden_units)
    flat_g = recv_g.reshape(slot_count, width)
    tile_rows = hidden_units // side
    tile_cols = width // side
    sub_rows = slot_count // side
    piece_h = (
        flat_h.reshape(side, sub_rows, side, tile_rows)
        .transpose(2, 0, 1, 3)
        .reshape(replicas, sub_rows, tile_rows)
    )
    piece_g = (
        flat_g.reshape(side, sub_rows, side, tile_cols)
        .transpose(0, 2, 1, 3)
        .reshape(replicas, sub_rows, tile_cols)
    )
    all_h, all_g = (
        lax.all_to_all(piece_h, "dp", split_axis=0, concat_axis=0, tiled=True),
        lax.all_to_all(piece_g, "dp", split_axis=0, concat_axis=0, tiled=True),
    )
    for bit in range(levels):
        partner_h = swapped(all_h, "dp", bit)
        all_h = join_pair(all_h, partner_h, replica, bit)
    for bit in range(levels, 2 * levels):
        partner_g = swapped(all_g, "dp", bit)
        all_g = join_pair(all_g, partner_g, replica, bit)
    tile_grad = lax.dot_general(
        all_h, all_g, (((0, 1), (0, 1)), ((), ())), preferred_element_type=jnp.float32
    )
    kept = jnp.sum(keep).astype(jnp.float32)
    factor = jnp.float32(replicas) / jnp.maximum(kept, jnp.float32(1.0))
    scaled = tile_grad * factor
    blocked = scaled.reshape(tile_rows, tile_cols // 128, 128)
    scales = jnp.max(jnp.abs(blocked), axis=-1)
    normed = (blocked / (scales[..., None] + 1e-06)).reshape(tile_rows, tile_cols)
    return (normed[None, None], scales[None, None])


def solution(mesh):
    placed = (
        P(("dp", "expert"), None),
        P(("dp", "expert"), None),
        P(("dp", "expert"), None),
        P(("dp", "expert"), None),
        P(),
    )
    return jax.shard_map(
        on_device,
        mesh=mesh,
        in_specs=placed,
        out_specs=(P("expert", "dp", None, None), P("expert", "dp", None, None)),
        check_vma=False,
    )
```

profile of v0, /device:TPU:0, one launch (start us, length us, event | category | flops | bytes accessed | tf_op | source)
XLA Modules:
  0.0 197.5 jit_solution(10361188149571825221)
XLA Ops:
  0.6 0.0 copy-start
  0.6 0.8 iota_compare_fusion
  1.4 0.8 reduce-window.8
  2.3 0.7 bitcast_subtract_fusion
  2.9 0.1 compare_select_fusion.1
  3.0 0.1 reshape.138
  3.1 1.4 gather_fusion
  4.5 0.1 gather.13
  4.6 0.1 reshape.146
  4.7 0.0 copy-done
  4.7 1.0 gather_fusion.1
  5.7 0.0 copy-start.5
  5.7 0.0 copy-start.4
  5.7 0.2 reshape.145
  5.9 1.0 broadcast_select_fusion
  6.9 4.3 %all-to-all-start = ((bf16[2,20,8192]{2,1,0:T(8,128)(2,1)}), bf16[2,20,8192]{2,1,0:T(8,128)(2,1)S(1)}, u32[]{:S(2)}, u32[]{:S(2)}) async-start(bf16[2,20,8192]{2,1,0:T(8,128)(2,1)} %broadcast_select_fusion), calls=%async_computation | async-start | bytes 1572864 | tf_op jit(solution)/shard_map/all_to_all | solution.py:52
  11.1 0.0 copy-done.5
  11.1 0.6 dynamic_slice.3
  12.4 0.0 copy-done.4
  12.4 0.8 gather_fusion.2
  13.3 0.1 reshape.153
  13.4 0.9 broadcast_select_fusion.1
  14.3 8.4 %all-to-all-done = bf16[2,20,8192]{2,1,0:T(8,128)(2,1)S(1)} async-done(((bf16[2,20,8192]{2,1,0:T(8,128)(2,1)}), bf16[2,20,8192]{2,1,0:T(8,128)(2,1)S(1)}, u32[]{:S(2)}, u32[]{:S(2)}) %all-to-all-start) | async-done | bytes 655392 | tf_op jit(solution)/shard_map/all_to_all | solution.py:52
  22.7 3.5 %all-to-all-start.2 = ((bf16[2,20,6144]{2,1,0:T(8,128)(2,1)}), bf16[2,20,6144]{2,1,0:T(8,128)(2,1)S(1)}, u32[]{:S(2)}, u32[]{:S(2)}) async-start(bf16[2,20,6144]{2,1,0:T(8,128)(2,1)} %broadcast_select_fusion.1), calls=%async_computation.2 | async-start | bytes 1179648 | tf_op jit(solution)/shard_map/all_to_all | solution.py:53
  26.2 0.4 reshape_reshape.6
  26.7 1.4 copy.40
  28.0 6.5 %all-to-all-done.2 = bf16[2,20,6144]{2,1,0:T(8,128)(2,1)S(1)} async-done(((bf16[2,20,6144]{2,1,0:T(8,128)(2,1)}), bf16[2,20,6144]{2,1,0:T(8,128)(2,1)S(1)}, u32[]{:S(2)}, u32[]{:S(2)}) %all-to-all-start.2) | async-done | bytes 491552 | tf_op jit(solution)/shard_map/all_to_all | solution.py:53
  34.6 5.9 %all-to-all-start.1 = ((bf16[16,10,2048]{2,1,0:T(8,128)(2,1)}), bf16[16,10,2048]{2,1,0:T(8,128)(2,1)S(1)}, u32[]{:S(2)}, u32[]{:S(2)}) async-start(bf16[16,10,2048]{2,1,0:T(8,128)(2,1)} %bitcast.5), calls=%async_computation.1 | async-start | bytes 2097152 | tf_op jit(solution)/shard_map/all_to_all | solution.py:72
  40.4 0.3 reshape_reshape.7
  40.7 1.0 copy.41
  41.8 21.6 %all-to-all-done.1 = bf16[16,10,2048]{2,1,0:T(8,128)(2,1)S(1)} async-done(((bf16[16,10,2048]{2,1,0:T(8,128)(2,1)}), bf16[16,10,2048]{2,1,0:T(8,128)(2,1)S(1)}, u32[]{:S(2)}, u32[]{:S(2)}) %all-to-all-start.1) | async-done | bytes 655392 | tf_op jit(solution)/shard_map/all_to_all | solution.py:72
  63.3 6.8 %all-to-all-start.3 = ((bf16[16,10,1536]{2,1,0:T(8,128)(2,1)}), bf16[16,10,1536]{2,1,0:T(8,128)(2,1)S(1)}, u32[]{:S(2)}, u32[]{:S(2)}) async-start(bf16[16,10,1536]{2,1,0:T(8,128)(2,1)} %bitcast.8), calls=%async_computation.3 | async-start | bytes 1572864 | tf_op jit(solution)/shard_map/all_to_all | solution.py:73
  70.1 1.2 copy.25
  71.3 0.4 collective-permute-start
  71.7 17.1 %all-to-all-done.3 = bf16[16,10,1536]{2,1,0:T(8,128)(2,1)S(1)} async-done(((bf16[16,10,1536]{2,1,0:T(8,128)(2,1)}), bf16[16,10,1536]{2,1,0:T(8,128)(2,1)S(1)}, u32[]{:S(2)}, u32[]{:S(2)}) %all-to-all-start.3) | async-done | bytes 491552 | tf_op jit(solution)/shard_map/all_to_all | solution.py:73
  88.8 0.3 copy.33
  89.1 2.1 %collective-permute-start.2 = (bf16[16,10,1536]{2,0,1:T(8,128)(2,1)S(1)}, bf16[16,10,1536]{2,0,1:T(8,128)(2,1)S(1)}, u32[]{:S(2)}, u32[]{:S(2)}) collective-permute-start(bf16[16,10,1536]{2,0,1:T(8,128)(2,1)S(1)} %copy.33), channel_id=1, source_target_pairs={{0,8},{8,0},{2,10},{10,2},{4,12},{12,4},{6,14},{14,6},{16,24},{24,... | collective-permute-start | bytes 1474568 | tf_op jit(solution)/shard_map/ppermute | solution.py:16
  91.2 0.0 collective-permute-done
  91.2 0.4 copy.26
  91.6 1.0 maximum_select_fusion.4
  92.6 0.0 copy-start.2
  92.6 1.1 copy-done.2
  93.7 1.8 copy.28
  95.6 1.6 collective-permute-start.1
  97.2 5.9 %collective-permute-done.2 = bf16[16,10,1536]{2,0,1:T(8,128)(2,1)S(1)} collective-permute-done((bf16[16,10,1536]{2,0,1:T(8,128)(2,1)S(1)}, bf16[16,10,1536]{2,0,1:T(8,128)(2,1)S(1)}, u32[]{:S(2)}, u32[]{:S(2)}) %collective-permute-start.2) | collective-permute-done | bytes 491552 | tf_op jit(solution)/shard_map/ppermute | solution.py:16
  103.0 0.3 copy.34
  103.3 0.8 maximum_select_fusion.5
  104.1 1.3 copy.36
  105.4 2.2 %collective-permute-start.3 = (bf16[16,20,1536]{2,0,1:T(8,128)(2,1)}, bf16[16,20,1536]{2,0,1:T(8,128)(2,1)S(1)}, u32[]{:S(2)}, u32[]{:S(2)}) collective-permute-start(bf16[16,20,1536]{2,0,1:T(8,128)(2,1)} %copy.36), channel_id=1, source_target_pairs={{0,16},{16,0},{2,18},{18,2},{4,20},{20,4},{6,22},{22,6},{8,24},{24... | collective-permute-start | bytes 2949128 | tf_op jit(solution)/shard_map/ppermute | solution.py:16
  107.6 0.6 reduce_sum.9
  108.9 0.0 copy-start.3
  108.9 42.8 %collective-permute-done.3 = bf16[16,20,1536]{2,0,1:T(8,128)(2,1)S(1)} collective-permute-done((bf16[16,20,1536]{2,0,1:T(8,128)(2,1)}, bf16[16,20,1536]{2,0,1:T(8,128)(2,1)S(1)}, u32[]{:S(2)}, u32[]{:S(2)}) %collective-permute-start.3) | collective-permute-done | bytes 983072 | tf_op jit(solution)/shard_map/ppermute | solution.py:16
  151.7 0.5 copy.37
  152.2 0.0 collective-permute-done.1
  152.3 2.0 %copy.29 = bf16[16,20,2048]{2,1,0:T(8,128)(2,1)S(1)} copy(bf16[16,20,2048]{2,0,1:T(8,128)(2,1)} %collective-permute-done.1) | data formatting | bytes 2621440 | tf_op jit(solution)/shard_map/ppermute | solution.py:16
  154.3 0.0 copy-done.3
  154.3 12.0 %fusion = (f32[2048,1536]{0,1:T(8,128)}, f32[2048,1536,1]{0,1,2:T(8,128)}) fusion(f32[]{:T(128)S(6)} %div.17, bf16[16,20,1536]{2,1,0:T(8,128)(2,1)S(1)} %copy.37, bf16[16,20,1536]{2,1,0:T(8,128)(2,1)S(1)} %maximum_select_fusion.5, pred[]{:T(512)S(6)} %eq.14, bf16[16,20,2048]{2,1,0:T(8,128)(2,1)S(1)} %copy.29, bf16[16,20,2048]{2,1,0:T(8,128)(2,1)S(1)} %copy-done.3, ...), kind=kOutput, calls=%fused_computation.5 | convolution fusion | flops 4053467136 | bytes 29753350 | tf_op jit(solution)/shard_map/dot_general | solution.py:81
  166.3 5.8 %reduce_max.9 = f32[2048,12]{0,1:T(8,128)S(1)} reduce(f32[2048,12,128]{0,2,1:T(8,128)} %bitcast.29, f32[]{:T(128)} %constant.37.clone.1), dimensions={2}, to_apply=%region_2.3 | reduce | flops 3121152 | bytes 12681220 | tf_op jit(solution)/shard_map/reduce_max | solution.py:88
  172.1 0.7 broadcast_in_dim.46
  172.9 12.0 %bitcast_divide_fusion = f32[2048,1536]{0,1:T(8,128)} fusion(f32[2048,1536,1]{0,1,2:T(8,128)} %get-tuple-element.13, f32[2048,12]{0,1:T(8,128)S(1)} %broadcast_add_fusion, f32[]{:T(128)S(6)} %div.17), kind=kLoop, calls=%fused_computation.3 | loop fusion | flops 6291456 | bytes 25264132 | tf_op jit(solution)/shard_map/div | solution.py:89
  184.9 0.0 copy-start.1
  184.9 12.7 %copy.39 = f32[1,1,2048,1536]{3,2,1,0:T(8,128)} copy(f32[1,1,2048,1536]{2,3,1,0:T(8,128)} %bitcast.28) | data formatting | bytes 25165824
  197.5 0.0 copy-done.1
  (5 shorter events, 0.1 us)
Async XLA Ops:
  0.6 4.1 %copy-start = (bf16[32,8192]{1,0:T(8,128)(2,1)S(1)}, bf16[32,8192]{1,0:T(8,128)(2,1)}, u32[]{:S(2)}) copy-start(bf16[32,8192]{1,0:T(8,128)(2,1)} %param.5) | copy-start | bytes 1572868
  5.7 5.5 %copy-start.5 = (s32[16]{0:T(128)S(1)}, s32[16]{0:T(128)}, u32[]{:S(2)}) copy-start(s32[16]{0:T(128)} %param.9) | copy-start | bytes 196
  5.7 6.7 %copy-start.4 = (bf16[32,6144]{1,0:T(8,128)(2,1)S(1)}, bf16[32,6144]{1,0:T(8,128)(2,1)}, u32[]{:S(2)}) copy-start(bf16[32,6144]{1,0:T(8,128)(2,1)} %param.6) | copy-start | bytes 1179652
  6.9 15.8 %all-to-all-start = ((bf16[2,20,8192]{2,1,0:T(8,128)(2,1)}), bf16[2,20,8192]{2,1,0:T(8,128)(2,1)S(1)}, u32[]{:S(2)}, u32[]{:S(2)}) async-start(bf16[2,20,8192]{2,1,0:T(8,128)(2,1)} %broadcast_select_fusion), calls=%async_computation | async-start | bytes 1572864 | tf_op jit(solution)/shard_map/all_to_all | solution.py:52
  22.7 11.9 %all-to-all-start.2 = ((bf16[2,20,6144]{2,1,0:T(8,128)(2,1)}), bf16[2,20,6144]{2,1,0:T(8,128)(2,1)S(1)}, u32[]{:S(2)}, u32[]{:S(2)}) async-start(bf16[2,20,6144]{2,1,0:T(8,128)(2,1)} %broadcast_select_fusion.1), calls=%async_computation.2 | async-start | bytes 1179648 | tf_op jit(solution)/shard_map/all_to_all | solution.py:53
  34.6 28.7 %all-to-all-start.1 = ((bf16[16,10,2048]{2,1,0:T(8,128)(2,1)}), bf16[16,10,2048]{2,1,0:T(8,128)(2,1)S(1)}, u32[]{:S(2)}, u32[]{:S(2)}) async-start(bf16[16,10,2048]{2,1,0:T(8,128)(2,1)} %bitcast.5), calls=%async_computation.1 | async-start | bytes 2097152 | tf_op jit(solution)/shard_map/all_to_all | solution.py:72
  63.3 25.5 %all-to-all-start.3 = ((bf16[16,10,1536]{2,1,0:T(8,128)(2,1)}), bf16[16,10,1536]{2,1,0:T(8,128)(2,1)S(1)}, u32[]{:S(2)}, u32[]{:S(2)}) async-start(bf16[16,10,1536]{2,1,0:T(8,128)(2,1)} %bitcast.8), calls=%async_computation.3 | async-start | bytes 1572864 | tf_op jit(solution)/shard_map/all_to_all | solution.py:73
  71.3 19.9 %collective-permute-start = (bf16[16,10,2048]{2,0,1:T(8,128)(2,1)}, bf16[16,10,2048]{2,0,1:T(8,128)(2,1)S(1)}, u32[]{:S(2)}, u32[]{:S(2)}) collective-permute-start(bf16[16,10,2048]{2,0,1:T(8,128)(2,1)} %copy.25), channel_id=1, source_target_pairs={{0,2},{2,0},{4,6},{6,4},{8,10},{10,8},{12,14},{14,12},{16,18},{18,... | collective-permute-start | bytes 1966088 | tf_op jit(solution)/shard_map/ppermute | solution.py:16
  89.1 14.0 %collective-permute-start.2 = (bf16[16,10,1536]{2,0,1:T(8,128)(2,1)S(1)}, bf16[16,10,1536]{2,0,1:T(8,128)(2,1)S(1)}, u32[]{:S(2)}, u32[]{:S(2)}) collective-permute-start(bf16[16,10,1536]{2,0,1:T(8,128)(2,1)S(1)} %copy.33), channel_id=1, source_target_pairs={{0,8},{8,0},{2,10},{10,2},{4,12},{12,4},{6,14},{14,6},{16,24},{24,... | collective-permute-start | bytes 1474568 | tf_op jit(solution)/shard_map/ppermute | solution.py:16
  92.6 1.1 copy-start.2
  95.6 56.7 %collective-permute-start.1 = (bf16[16,20,2048]{2,0,1:T(8,128)(2,1)}, bf16[16,20,2048]{2,0,1:T(8,128)(2,1)}, u32[]{:S(2)}, u32[]{:S(2)}) collective-permute-start(bf16[16,20,2048]{2,0,1:T(8,128)(2,1)} %copy.28), channel_id=1, source_target_pairs={{0,4},{4,0},{2,6},{6,2},{8,12},{12,8},{10,14},{14,10},{16,20},{20,... | collective-permute-start | bytes 3932168 | tf_op jit(solution)/shard_map/ppermute | solution.py:16
  105.4 46.3 %collective-permute-start.3 = (bf16[16,20,1536]{2,0,1:T(8,128)(2,1)}, bf16[16,20,1536]{2,0,1:T(8,128)(2,1)S(1)}, u32[]{:S(2)}, u32[]{:S(2)}) collective-permute-start(bf16[16,20,1536]{2,0,1:T(8,128)(2,1)} %copy.36), channel_id=1, source_target_pairs={{0,16},{16,0},{2,18},{18,2},{4,20},{20,4},{6,22},{22,6},{8,24},{24... | collective-permute-start | bytes 2949128 | tf_op jit(solution)/shard_map/ppermute | solution.py:16
  108.9 45.4 %copy-start.3 = (bf16[16,20,2048]{2,1,0:T(8,128)(2,1)S(1)}, bf16[16,20,2048]{2,1,0:T(8,128)(2,1)}, u32[]{:S(2)}) copy-start(bf16[16,20,2048]{2,1,0:T(8,128)(2,1)} %copy-done.2) | copy-start | bytes 3932164
  184.9 12.7 %copy-start.1 = (bf16[32,8192]{1,0:T(8,128)(2,1)S(1)}, bf16[32,8192]{1,0:T(8,128)(2,1)}, u32[]{:S(2)}) copy-start(bf16[32,8192]{1,0:T(8,128)(2,1)} %param.5) | copy-start | bytes 1572868
where the time goes:
time: 198 us
  waiting for transfers between devices  102 us (52%)
  local copies, waits for them, and re-layouts  29.8 us (15%)
  starting transfers between devices  26.7 us (13%)
  other arithmetic  24.6 us (12%)
  matrix products  12 us (6%)
  between operations  2.18 us (1%)
    ppermute x4, waiting for transfers between devices, swapped(): return lax.ppermute(block, axis, route)  48.7 us
    all_to_all x1, waiting for transfers between devices, on_device(): lax.all_to_all(piece_h, 'dp', split_axis=0, concat_axis=0, tiled=True)  21.6 us
    all_to_all x1, waiting for transfers between devices, on_device(): lax.all_to_all(piece_g, 'dp', split_axis=0, concat_axis=0, tiled=True)  17.1 us
    unnamed x13, local copies, waits for them, and re-layouts  13.8 us
    div x1, other arithmetic, on_device(): blocked / (scales[..., None] + 1e-06)  12 us
    dot_general x1, matrix products, on_device(): lax.dot_general(all_h, all_g, (((0, 1), (0, 1)), ((), ())), preferred_ele...  12 us
    all_to_all x1, waiting for transfers between devices, on_device(): lax.all_to_all(send_h, 'expert', split_axis=0, concat_axis=0, tiled=True)  8.4 us
    all_to_all x1, starting transfers between devices, on_device(): lax.all_to_all(piece_g, 'dp', split_axis=0, concat_axis=0, tiled=True)  6.8 us
  transfers between devices with their start and end apart: 8, of which 6 were waited for; matrix products, arithmetic and copies ran while one was open for 7% of the time, Pallas kernels for 0%

commit v1 on v0

v1 whole, which is shorter than its diff:
```python
import functools
import math

import jax
import jax.numpy as jnp
from jax import lax
from jax.experimental import pallas as pl
from jax.experimental.pallas import tpu as pltpu
from jax.sharding import PartitionSpec as P

MESH = pl.DeviceIdType.MESH
LANES = 128
SUB = 16


def swapped(block, axis, bit):
    count = lax.axis_size(axis)
    route = []
    for low in range(count):
        high = low | 1 << bit
        if high != low and high < count:
            route += [(low, high), (high, low)]
    return lax.ppermute(block, axis, route)


def build_slots(rows_dev, counts_dev, perm_dev, capacity):
    offsets = jnp.cumsum(counts_dev) - counts_dev
    slots = jnp.arange(capacity, dtype=jnp.int32)
    position = offsets[:, None] + slots[None, :]
    position = jnp.minimum(position, rows_dev.shape[0] - 1)
    live = slots[None, :] < counts_dev[:, None]
    local = perm_dev[position]
    picked = rows_dev[local]
    return jnp.where(live[:, :, None], picked, jnp.zeros_like(picked))


def join_pair(mine, partner, replica, bit):
    lower = replica >> bit & 1 == 0
    first = jnp.concatenate([mine, partner], axis=1)
    second = jnp.concatenate([partner, mine], axis=1)
    return jnp.where(lower, first, second)


def gather_general(hidden, out_grad, counts, route_index, keep, capacity):
    experts = lax.axis_size("expert")
    replicas = lax.axis_size("dp")
    side = math.isqrt(replicas)
    levels = side.bit_length() - 1
    replica = lax.axis_index("dp")
    hidden_units = hidden.shape[1]
    width = out_grad.shape[1]
    grad_rows = jnp.where(keep[replica] > 0, out_grad, jnp.zeros_like(out_grad))
    send_h = build_slots(hidden, counts[0], route_index[0], capacity)
    send_g = build_slots(grad_rows, counts[0], route_index[0], capacity)
    recv_h = lax.all_to_all(send_h, "expert", split_axis=0, concat_axis=0, tiled=True)
    recv_g = lax.all_to_all(send_g, "expert", split_axis=0, concat_axis=0, tiled=True)
    slot_count = experts * capacity
    tile_rows = hidden_units // side
    tile_cols = width // side
    sub_rows = slot_count // side
    piece_h = (
        recv_h.reshape(side, sub_rows, side, tile_rows)
        .transpose(2, 0, 1, 3)
        .reshape(replicas, sub_rows, tile_rows)
    )
    piece_g = (
        recv_g.reshape(side, sub_rows, side, tile_cols)
        .transpose(0, 2, 1, 3)
        .reshape(replicas, sub_rows, tile_cols)
    )
    all_h = lax.all_to_all(piece_h, "dp", split_axis=0, concat_axis=0, tiled=True)
    all_g = lax.all_to_all(piece_g, "dp", split_axis=0, concat_axis=0, tiled=True)
    for bit in range(levels):
        all_h = join_pair(all_h, swapped(all_h, "dp", bit), replica, bit)
    for bit in range(levels, 2 * levels):
        all_g = join_pair(all_g, swapped(all_g, "dp", bit), replica, bit)
    return [(all_h.reshape(-1, tile_rows), all_g.reshape(-1, tile_cols))]


def slots_kernel(side, big, rest, counts, keep, route, hidden, grad, h_o, h_c, g_o, g_c):
    me = lax.axis_index("expert")
    rows = hidden.shape[0]
    total = 2 * big + 4 * rest
    row = lax.broadcasted_iota(jnp.int32, (total, rows), 0)
    pos = lax.broadcasted_iota(jnp.int32, (total, rows), 1)
    tail = row >= 2 * big
    in_tail = row - 2 * big
    other = jnp.logical_or(
        in_tail >= 2 * rest, jnp.logical_and(row >= big, jnp.logical_not(tail))
    )
    tail_row = jnp.where(in_tail >= 2 * rest, in_tail - 2 * rest, in_tail) - me * rest
    slot = jnp.where(tail, big + tail_row, jnp.where(row >= big, row - big, row))
    valid = jnp.logical_or(
        jnp.logical_not(tail), jnp.logical_and(tail_row >= 0, tail_row < rest)
    )
    first, second = counts[0, 0], counts[0, 1]
    expert = jnp.where(other, 1 - me, me)
    start = jnp.where(expert == 0, 0, first)
    count = jnp.where(expert == 0, first, second)
    take = jnp.logical_and(valid, jnp.logical_and(slot < count, pos == start + slot))
    take = jnp.where(take, 1.0, 0.0).astype(jnp.bfloat16)
    local = lax.broadcasted_iota(jnp.int32, (rows, rows), 0)
    perm = jnp.where(local == route[...], 1.0, 0.0).astype(jnp.bfloat16)
    pick = lax.dot_general(
        take, perm, (((1,), (1,)), ((), ())), preferred_element_type=jnp.float32
    )
    kept = keep[lax.axis_index("dp")] > 0
    pick_h = pick.astype(jnp.bfloat16)
    pick_g = jnp.where(kept, pick, 0.0).astype(jnp.bfloat16)
    for pick_x, src, o_ref, c_ref in ((pick_h, hidden, h_o, h_c), (pick_g, grad, g_o, g_c)):
        cols = o_ref.shape[3]
        for part in range(side):
            got = jnp.dot(
                pick_x,
                src[:, part * cols : (part + 1) * cols],
                preferred_element_type=jnp.float32,
            ).astype(jnp.bfloat16)
            for k in range(2):
                o_ref[k, part] = got[k * big : (k + 1) * big]
                low = 2 * big + 2 * rest * k
                c_ref[k, part] = got[low : low + 2 * rest]


def spread_kernel(
    n, h_o, h_c, g_o, g_c, hh, hc, gg, gc, ph, phc, pg, pgc, sh, sg,
    send_sem, h_sem, g_sem, y_sem, own_sem,
):
    here = lax.axis_index("dp")
    y = lax.axis_index("expert")
    z, q = here // n, here % n
    zs = [(z + d) % n for d in range(n)]
    qs = [(q + d) % n for d in range(n)]

    barrier = pltpu.get_barrier_semaphore()
    peers = [(here, 1 - y)]
    peers += [(zs[d] * n + q, y) for d in range(1, n)]
    peers += [(z * n + qs[d], y) for d in range(1, n)]
    for peer in peers:
        pl.semaphore_signal(barrier, inc=1, device_id=peer, device_id_type=MESH)
    pl.semaphore_wait(barrier, len(peers))

    ends = []

    def send(src, dst, sem, peer, when=None):
        copy = pltpu.make_async_remote_copy(
            src_ref=src,
            dst_ref=dst,
            send_sem=send_sem.at[len(ends)],
            recv_sem=sem,
            device_id=peer,
            device_id_type=MESH,
        )
        ends.append((copy, when))
        if when is None:
            copy.start()
        else:
            pl.when(when)(copy.start)

    def landed(view, sem):
        pltpu.make_async_copy(view, view, sem).wait()

    h_at = lambda i, b: hh.at[i, b] if b < 2 else hc.at[i]
    g_at = lambda i, b: gg.at[i, b] if b < 2 else gc.at[i]
    h_from = lambda b, i: (h_o.at[0, i], ph.at[i], sh.at[i])[b]
    g_from = lambda b, i: (g_o.at[0, i], pg.at[i], sg.at[i])[b]
    hs = lambda i, b: h_sem.at[i * 3 + b]
    gs = lambda i, b: g_sem.at[i * 3 + b]
    own = []

    def keep_own(src, dst):
        copy = pltpu.make_async_copy(src, dst, own_sem.at[len(own)])
        copy.start()
        own.append(copy)

    def fan_h(src, i, b):
        for d in range(1, n):
            send(src, h_at(i, b), hs(i, b), (z * n + qs[d], y))

    def up_g(src, i, b, ok=None):
        when = z + 1 < n
        when = when if ok is None else jnp.logical_and(when, ok)
        send(src, g_at(i, b), gs(i, b), (jnp.minimum(z + 1, n - 1) * n + q, y), when)

    def down_g(src, i, b, ok=None):
        when = z >= 1
        when = when if ok is None else jnp.logical_and(when, ok)
        send(src, g_at(i, b), gs(i, b), (jnp.maximum(z - 1, 0) * n + q, y), when)

    def start_block(b):
        for d in range(1, n):
            send(g_from(b, qs[d]), g_at(here, b), gs(here, b), (z * n + qs[d], y))
        for d in range(1, n):
            send(h_from(b, zs[d]), h_at(here, b), hs(here, b), (zs[d] * n + q, y))
        fan_h(h_from(b, z), here, b)
        up_g(g_from(b, q), here, b)
        down_g(g_from(b, q), here, b)
        keep_own(h_from(b, z), h_at(here, b))
        keep_own(g_from(b, q), g_at(here, b))

    def plane_g(b):
        for d in range(1, n):
            i = z * n + qs[d]
            landed(g_at(i, b), gs(i, b))
            up_g(g_at(i, b), i, b)
            down_g(g_at(i, b), i, b)

    def arrive_h(b):
        for d in range(1, n):
            i = zs[d] * n + q
            landed(h_at(i, b), hs(i, b))
            fan_h(h_at(i, b), i, b)

    def forward_g(b, d):
        for k in range(n):
            low = jnp.maximum(z - d, 0) * n + k
            high = jnp.minimum(z + d, n - 1) * n + k

            @pl.when(z - d >= 0)
            def _():
                landed(g_at(low, b), gs(low, b))

            if d < n - 1:
                up_g(g_at(low, b), low, b, z - d >= 0)

            @pl.when(z + d < n)
            def _():
                landed(g_at(high, b), gs(high, b))

            if d < n - 1:
                down_g(g_at(high, b), high, b, z + d < n)

    def partner(b):
        if b == 1:
            for i in range(n):
                landed(ph.at[i], y_sem.at[i])
                landed(pg.at[i], y_sem.at[n + i])
        else:
            landed(phc, y_sem.at[2 * n])
            landed(pgc, y_sem.at[2 * n + 1])
            sh[...] = h_c[0] + phc[...]
            sg[...] = g_c[0] + pgc[...]

    across = (here, 1 - y)
    for i in range(n):
        send(g_o.at[1, i], pg.at[i], y_sem.at[n + i], across)
        send(h_o.at[1, i], ph.at[i], y_sem.at[i], across)
    send(h_c.at[1], phc, y_sem.at[2 * n], across)
    send(g_c.at[1], pgc, y_sem.at[2 * n + 1], across)
    start_block(0)
    plane_g(0)
    partner(1)
    start_block(1)
    arrive_h(0)
    plane_g(1)
    forward_g(0, 1)
    partner(2)
    arrive_h(1)
    start_block(2)
    forward_g(1, 1)
    forward_g(0, 2)
    plane_g(2)
    arrive_h(2)
    for d in range(1, n):
        for b in range(3):
            if (b, d) not in ((0, 1), (1, 1), (0, 2)):
                forward_g(b, d)
    for b in range(3):
        for d in range(1, n):
            for zz in range(n):
                i = zz * n + qs[d]
                landed(h_at(i, b), hs(i, b))
    for copy in own:
        copy.wait()
    for copy, when in ends:
        if when is None:
            copy.wait_send()
        else:
            pl.when(when)(copy.wait_send)


def n_sends(n):
    block = 2 * (n - 1) + (n - 1) + 2
    plane = 2 * (n - 1)
    arrive = (n - 1) * (n - 1)
    forward = (n - 2) * n * 2
    return 2 * n + 2 + 3 * (block + plane + arrive + forward)


def gather_pairs(hidden, out_grad, counts, route_index, keep, capacity):
    replicas = lax.axis_size("dp")
    n = math.isqrt(replicas)
    hcols, gcols = hidden.shape[1] // n, out_grad.shape[1] // n
    big = capacity // SUB * SUB
    rest = capacity - big
    kind = jnp.bfloat16
    vmem = pl.BlockSpec(memory_space=pltpu.VMEM)
    smem = pl.BlockSpec(memory_space=pltpu.SMEM)
    made = pl.pallas_call(
        functools.partial(slots_kernel, n, big, rest),
        out_shape=[
            jax.ShapeDtypeStruct((2, n, big, hcols), kind),
            jax.ShapeDtypeStruct((2, n, 2 * rest, hcols), kind),
            jax.ShapeDtypeStruct((2, n, big, gcols), kind),
            jax.ShapeDtypeStruct((2, n, 2 * rest, gcols), kind),
        ],
        in_specs=[smem, smem, vmem, vmem, vmem],
        out_specs=[vmem] * 4,
        name="slots",
    )(counts, keep, route_index, hidden, out_grad)
    hh, hc, gg, gc = pl.pallas_call(
        functools.partial(spread_kernel, n),
        out_shape=[
            jax.ShapeDtypeStruct((replicas, 2, big, hcols), kind),
            jax.ShapeDtypeStruct((replicas, 2 * rest, hcols), kind),
            jax.ShapeDtypeStruct((replicas, 2, big, gcols), kind),
            jax.ShapeDtypeStruct((replicas, 2 * rest, gcols), kind),
        ],
        in_specs=[vmem] * 4,
        out_specs=[vmem] * 4,
        scratch_shapes=[
            pltpu.VMEM((n, big, hcols), kind),
            pltpu.VMEM((n, 2 * rest, hcols), kind),
            pltpu.VMEM((n, big, gcols), kind),
            pltpu.VMEM((n, 2 * rest, gcols), kind),
            pltpu.VMEM((n, 2 * rest, hcols), kind),
            pltpu.VMEM((n, 2 * rest, gcols), kind),
            pltpu.SemaphoreType.DMA((n_sends(n),)),
            pltpu.SemaphoreType.DMA((replicas * 3,)),
            pltpu.SemaphoreType.DMA((replicas * 3,)),
            pltpu.SemaphoreType.DMA((2 * n + 2,)),
            pltpu.SemaphoreType.DMA((6,)),
        ],
        compiler_params=pltpu.CompilerParams(collective_id=0, has_side_effects=True),
        name="spread",
    )(*made)
    return [
        (hh.reshape(-1, hcols), gg.reshape(-1, gcols)),
        (hc.reshape(-1, hcols), gc.reshape(-1, gcols)),
    ]


def tile_kernel(pairs, keep, *refs):
    out, scales = refs[2 * pairs :]
    replicas = keep.shape[0]
    kept = keep[0]
    for i in range(1, replicas):
        kept = kept + keep[i]
    factor = jnp.float32(replicas) / jnp.maximum(
        jnp.full((1, LANES), kept, jnp.int32).astype(jnp.float32), 1.0
    )
    total = None
    for i in range(pairs):
        term = lax.dot_general(
            refs[2 * i][...],
            refs[2 * i + 1][...],
            (((0,), (0,)), ((), ())),
            preferred_element_type=jnp.float32,
        )
        total = term if total is None else total + term
    tops = []
    for b in range(out.shape[1] // LANES):
        block = total[:, b * LANES : (b + 1) * LANES] * factor
        top = jnp.max(jnp.abs(block), axis=1, keepdims=True)
        out[:, b * LANES : (b + 1) * LANES] = block * (1.0 / (top + 1e-6))
        tops.append(top)
    scales[...] = jnp.concatenate(tops, axis=1)


def tile_grad(pairs, keep):
    rows, cols = pairs[0][0].shape[1], pairs[0][1].shape[1]
    step = min(rows, 256)
    args, specs = [], []
    for h, g in pairs:
        args += [h, g]
        specs.append(pl.BlockSpec((h.shape[0], step), lambda i: (0, i)))
        specs.append(pl.BlockSpec((g.shape[0], cols), lambda i: (0, 0)))
    return pl.pallas_call(
        functools.partial(tile_kernel, len(pairs)),
        grid=(rows // step,),
        out_shape=[
            jax.ShapeDtypeStruct((rows, cols), jnp.float32),
            jax.ShapeDtypeStruct((rows, cols // LANES), jnp.float32),
        ],
        in_specs=[pl.BlockSpec(memory_space=pltpu.SMEM)] + specs,
        out_specs=[
            pl.BlockSpec((step, cols), lambda i: (i, 0)),
            pl.BlockSpec((step, cols // LANES), lambda i: (i, 0)),
        ],
        name="tile_grad",
    )(keep, *args)


def on_device(hidden, out_grad, counts, route_index, keep):
    experts = lax.axis_size("expert")
    tok_rows = hidden.shape[0]
    capacity = max(tok_rows // 4, tok_rows // experts + 4)
    rest = capacity % SUB
    paired = experts == 2 and capacity == SUB + rest and 2 * rest == SUB // 2
    gather = gather_pairs if paired else gather_general
    pairs = gather(hidden, out_grad, counts, route_index, keep, capacity)
    normed, scales = tile_grad(pairs, keep)
    return (normed[None, None], scales[None, None])


def solution(mesh):
    placed = (
        P(("dp", "expert"), None),
        P(("dp", "expert"), None),
        P(("dp", "expert"), None),
        P(("dp", "expert"), None),
        P(),
    )
    return jax.shard_map(
        on_device,
        mesh=mesh,
        in_specs=placed,
        out_specs=(P("expert", "dp", None, None), P("expert", "dp", None, None)),
        check_vma=False,
    )
```

time: 198 us -> 77.7 us (0.39)
  waiting for transfers between devices: 102 us -> 0 us
  Pallas kernels: 0 us -> 74.4 us
  local copies, waits for them, and re-layouts: 29.8 us -> 2.2 us
  starting transfers between devices: 26.7 us -> 0 us
  other arithmetic: 24.6 us -> 0 us
  matrix products: 12 us -> 0 us
    pallas_call x0 -> x3, Pallas kernels: none -> 74.4 us  [the longest x1 60.2 us: gather_pairs(): pl.pallas_call(functools.partial(spread_kernel, n), out_shape=[jax.ShapeD...]
    all_to_all x4 -> x0, waiting for transfers between devices: 53.6 us -> none  [the longest x1 21.6 us: on_device(): lax.all_to_all(piece_h, 'dp', split_axis=0, concat_axis=0, tiled=True)]
    ppermute x4 -> x0, waiting for transfers between devices: 48.7 us -> none  [swapped(): return lax.ppermute(block, axis, route)]
    all_to_all x4 -> x0, starting transfers between devices: 20.4 us -> none  [the longest x1 6.8 us: on_device(): lax.all_to_all(piece_g, 'dp', split_axis=0, concat_axis=0, tiled=True)]
    div x1 -> x0, other arithmetic: 12 us -> none  [on_device(): blocked / (scales[..., None] + 1e-06)]
    dot_general x1 -> x0, matrix products: 12 us -> none  [on_device(): lax.dot_general(all_h, all_g, (((0, 1), (0, 1)), ((), ())), preferred_ele...]
    unnamed x13 -> x1, local copies, waits for them, and re-layouts: 13.8 us -> 2.2 us
    ppermute x4 -> x0, starting transfers between devices: 6.31 us -> none  [swapped(): return lax.ppermute(block, axis, route)]
  transfers between devices with their start and end apart: 8 -> 0, of which waited for: 6 -> 0; matrix products, arithmetic and copies ran while one was open for 7% -> 0% of each run, Pallas kernels for 0% -> 0%
where the time goes in v1:
time: 77.7 us; the launch traced here: 77.3 us
  Pallas kernels  74.4 us (96%)
  local copies, waits for them, and re-layouts  2.2 us (3%)
    pallas_call x1, Pallas kernels, gather_pairs(): pl.pallas_call(functools.partial(spread_kernel, n), out_shape=[jax.ShapeD...  60.2 us
    pallas_call x1, Pallas kernels, tile_grad(): pl.pallas_call(functools.partial(tile_kernel, len(pairs)), grid=(rows //...  11.5 us
    pallas_call x1, Pallas kernels, gather_pairs(): pl.pallas_call(functools.partial(slots_kernel, n, big, rest), out_shape=[...  2.72 us
    unnamed x1, local copies, waits for them, and re-layouts  2.2 us

profile of v1, /device:TPU:0, one launch (start us, length us, event | category | flops | bytes accessed | tf_op | source)
XLA Modules:
  0.0 77.3 jit_solution(242824992724257221)
XLA Ops:
  0.6 2.7 %slots.1 = (bf16[2,4,16,2048]{3,2,1,0:T(8,128)(2,1)}, bf16[2,4,8,2048]{3,2,1,0:T(8,128)(2,1)}, bf16[2,4,16,1536]{3,2,1,0:T(8,128)(2,1)}, bf16[2,4,8,1536]{3,2,1,0:T(8,128)(2,1)}) custom-call(s32[1,2]{1,0:T(1,128)} %counts.1, s32[16]{0:T(128)} %keep.3, s32[1,32]{1,0:T(1,128)} %route.1, bf16[32,8192]{1,0:T(8,128)(2,1)} %hidden.1, bf16[32,6144]{1,0:T(8,128)(2,1)} %grad.1), custom_call_target="tpu_custom_call" | custom-call | tf_op jit(solution)/shard_map/slots/pallas_call | solution.py:298
  3.4 60.2 %spread.1 = (bf16[16,2,16,2048]{3,2,1,0:T(8,128)(2,1)}, bf16[16,8,2048]{2,1,0:T(8,128)(2,1)}, bf16[16,2,16,1536]{3,2,1,0:T(8,128)(2,1)}, bf16[16,8,1536]{2,1,0:T(8,128)(2,1)}) custom-call(bf16[2,4,16,2048]{3,2,1,0:T(8,128)(2,1)} %get-tuple-element.12.h_o, bf16[2,4,8,2048]{3,2,1,0:T(8,128)(2,1)} %get-tuple-element.13.h_c, ...), custom_call_target="tpu_custom_call" | custom-call | tf_op jit(solution)/shard_map/spread/pallas_call | solution.py:310
  63.6 11.5 %tile_grad.1 = (f32[2048,1536]{1,0:T(8,128)}, f32[2048,12]{1,0:T(8,128)}) custom-call(s32[16]{0:T(128)} %keep.3, bf16[512,2048]{1,0:T(8,128)(2,1)} %bitcast.6, bf16[512,1536]{1,0:T(8,128)(2,1)} %bitcast.7, bf16[128,2048]{1,0:T(8,128)(2,1)} %bitcast.9, bf16[128,1536]{1,0:T(8,128)(2,1)} %bitcast.10), custom_call_target="tpu_custom_call" | custom-call | tf_op jit(solution)/shard_map/tile_grad/pallas_call | solution.py:377
  75.1 2.2 %copy.7 = f32[1,1,2048,12]{2,1,3,0:T(1,128)} copy(f32[1,1,2048,12]{3,2,1,0:T(8,128)} %bitcast.8) | data formatting | bytes 196608

commit v2 on v1

--- a/solution.py
+++ b/solution.py
@@ -123,11 +123,14 @@
 
 def spread_kernel(
     n, h_o, h_c, g_o, g_c, hh, hc, gg, gc, ph, phc, pg, pgc, sh, sg,
-    send_sem, h_sem, g_sem, y_sem, own_sem,
+    send_sem, h1_sem, h2_sem, g1_sem, g2_sem, y_sem, own_sem,
 ):
     here = lax.axis_index("dp")
     y = lax.axis_index("expert")
     z, q = here // n, here % n
+    twin = q + 1 - 2 * (q % 2)
+    over = (q + n // 2) % n
+    far = (twin + n // 2) % n
     zs = [(z + d) % n for d in range(n)]
     qs = [(q + d) % n for d in range(n)]
 
@@ -159,118 +162,111 @@
     def landed(view, sem):
         pltpu.make_async_copy(view, view, sem).wait()
 
-    h_at = lambda i, b: hh.at[i, b] if b < 2 else hc.at[i]
-    g_at = lambda i, b: gg.at[i, b] if b < 2 else gc.at[i]
+    h_at = lambda i, k, b: hh.at[i, k, b] if b < 2 else hc.at[i, k]
+    g_at = lambda i, k, b: gg.at[i, k, b] if b < 2 else gc.at[i, k]
+    h_all = lambda k, b: hh.at[:, k, b] if b < 2 else hc.at[:, k]
+    g_all = lambda i, b: gg.at[i, :, b] if b < 2 else gc.at[i]
     h_from = lambda b, i: (h_o.at[0, i], ph.at[i], sh.at[i])[b]
     g_from = lambda b, i: (g_o.at[0, i], pg.at[i], sg.at[i])[b]
-    hs = lambda i, b: h_sem.at[i * 3 + b]
-    gs = lambda i, b: g_sem.at[i * 3 + b]
-    own = []
-
-    def keep_own(src, dst):
-        copy = pltpu.make_async_copy(src, dst, own_sem.at[len(own)])
-        copy.start()
-        own.append(copy)
-
-    def fan_h(src, i, b):
+
+    def own_h(b):
+        return pltpu.make_async_copy(h_from(b, z), h_at(z, q, b), own_sem.at[2 * b])
+
+    def own_g(b):
+        return pltpu.make_async_copy(g_from(b, q), g_at(z, q, b), own_sem.at[2 * b + 1])
+
+    def start_g(b):
         for d in range(1, n):
-            send(src, h_at(i, b), hs(i, b), (z * n + qs[d], y))
-
-    def up_g(src, i, b, ok=None):
-        when = z + 1 < n
-        when = when if ok is None else jnp.logical_and(when, ok)
-        send(src, g_at(i, b), gs(i, b), (jnp.minimum(z + 1, n - 1) * n + q, y), when)
-
-    def down_g(src, i, b, ok=None):
-        when = z >= 1
-        when = when if ok is None else jnp.logical_and(when, ok)
-        send(src, g_at(i, b), gs(i, b), (jnp.maximum(z - 1, 0) * n + q, y), when)
-
-    def start_block(b):
+            peer = (z * n + qs[d], y)
+            send(g_from(b, qs[d]), g_at(z, q, b), g1_sem.at[b * n + q], peer)
+        own_g(b).start()
+
+    def start_h(b):
         for d in range(1, n):
-            send(g_from(b, qs[d]), g_at(here, b), gs(here, b), (z * n + qs[d], y))
+            peer = (zs[d] * n + q, y)
+            send(h_from(b, zs[d]), h_at(z, q, b), h1_sem.at[b * n + z], peer)
+        own_h(b).start()
+
+    def up_g(i, b, when):
+        peer = (jnp.minimum(z + 1, n - 1) * n + q, y)
+        send(g_all(i, b), g_all(i, b), g2_sem.at[b * n + i], peer, when)
+
+    def down_g(i, b, when):
+        peer = (jnp.maximum(z - 1, 0) * n + q, y)
+        send(g_all(i, b), g_all(i, b), g2_sem.at[b * n + i], peer, when)
+
+    def plane_g(b):
+        own_g(b).wait()
         for d in range(1, n):
-            send(h_from(b, zs[d]), h_at(here, b), hs(here, b), (zs[d] * n + q, y))
-        fan_h(h_from(b, z), here, b)
-        up_g(g_from(b, q), here, b)
-        down_g(g_from(b, q), here, b)
-        keep_own(h_from(b, z), h_at(here, b))
-        keep_own(g_from(b, q), g_at(here, b))
-
-    def plane_g(b):
+            landed(g_at(z, qs[d], b), g1_sem.at[b * n + qs[d]])
+        up_g(z, b, z + 1 < n)
+        down_g(z, b, z >= 1)
+
+    def forward_g(b, d):
+        low = jnp.maximum(z - d, 0)
+        high = jnp.minimum(z + d, n - 1)
+
+        @pl.when(z - d >= 0)
+        def _():
+            landed(g_all(low, b), g2_sem.at[b * n + low])
+
+        if d < n - 1:
+            up_g(low, b, jnp.logical_and(z + 1 < n, z - d >= 0))
+
+        @pl.when(z + d < n)
+        def _():
+            landed(g_all(high, b), g2_sem.at[b * n + high])
+
+        if d < n - 1:
+            down_g(high, b, jnp.logical_and(z >= 1, z + d < n))
+
+    def fan_h(b):
+        own_h(b).wait()
         for d in range(1, n):
-            i = z * n + qs[d]
-            landed(g_at(i, b), gs(i, b))
-            up_g(g_at(i, b), i, b)
-            down_g(g_at(i, b), i, b)
-
-    def arrive_h(b):
-        for d in range(1, n):
-            i = zs[d] * n + q
-            landed(h_at(i, b), hs(i, b))
-            fan_h(h_at(i, b), i, b)
-
-    def forward_g(b, d):
-        for k in range(n):
-            low = jnp.maximum(z - d, 0) * n + k
-            high = jnp.minimum(z + d, n - 1) * n + k
-
-            @pl.when(z - d >= 0)
-            def _():
-                landed(g_at(low, b), gs(low, b))
-
-            if d < n - 1:
-                up_g(g_at(low, b), low, b, z - d >= 0)
-
-            @pl.when(z + d < n)
-            def _():
-                landed(g_at(high, b), gs(high, b))
-
-            if d < n - 1:
-                down_g(g_at(high, b), high, b, z + d < n)
-
-    def partner(b):
-        if b == 1:
-            for i in range(n):
-                landed(ph.at[i], y_sem.at[i])
-                landed(pg.at[i], y_sem.at[n + i])
-        else:
-            landed(phc, y_sem.at[2 * n])
-            landed(pgc, y_sem.at[2 * n + 1])
-            sh[...] = h_c[0] + phc[...]
-            sg[...] = g_c[0] + pgc[...]
+            landed(h_at(zs[d], q, b), h1_sem.at[b * n + zs[d]])
+        for to in (over, twin):
+            send(h_all(q, b), h_all(q, b), h2_sem.at[b * n + q], (z * n + to, y))
+
+    def relay_h(b):
+        landed(h_all(over, b), h2_sem.at[b * n + over])
+        send(h_all(over, b), h_all(over, b), h2_sem.at[b * n + over], (z * n + twin, y))
 
     across = (here, 1 - y)
-    for i in range(n):
-        send(g_o.at[1, i], pg.at[i], y_sem.at[n + i], across)
-        send(h_o.at[1, i], ph.at[i], y_sem.at[i], across)
-    send(h_c.at[1], phc, y_sem.at[2 * n], across)
-    send(g_c.at[1], pgc, y_sem.at[2 * n + 1], across)
-    start_block(0)
+    start_g(0)
+    start_h(0)
+    send(g_o.at[1], pg, y_sem.at[0], across)
+    send(h_o.at[1], ph, y_sem.at[1], across)
+    send(g_c.at[1], pgc, y_sem.at[2], across)
+    send(h_c.at[1], phc, y_sem.at[3], across)
     plane_g(0)
-    partner(1)
-    start_block(1)
-    arrive_h(0)
+    fan_h(0)
+    landed(pg, y_sem.at[0])
+    start_g(1)
+    forward_g(0, 1)
+    landed(ph, y_sem.at[1])
+    start_h(1)
     plane_g(1)
-    forward_g(0, 1)
-    partner(2)
-    arrive_h(1)
-    start_block(2)
+    forward_g(0, 2)
+    relay_h(0)
+    landed(pgc, y_sem.at[2])
+    landed(phc, y_sem.at[3])
+    sg[...] = g_c[0] + pgc[...]
+    sh[...] = h_c[0] + phc[...]
+    fan_h(1)
+    start_g(2)
+    start_h(2)
     forward_g(1, 1)
-    forward_g(0, 2)
     plane_g(2)
-    arrive_h(2)
-    for d in range(1, n):
-        for b in range(3):
-            if (b, d) not in ((0, 1), (1, 1), (0, 2)):
-                forward_g(b, d)
+    relay_h(1)
+    fan_h(2)
+    forward_g(1, 2)
+    forward_g(2, 1)
+    relay_h(2)
+    forward_g(2, 2)
     for b in range(3):
-        for d in range(1, n):
-            for zz in range(n):
-                i = zz * n + qs[d]
-                landed(h_at(i, b), hs(i, b))
-    for copy in own:
-        copy.wait()
+        forward_g(b, n - 1)
+        for k in (twin, far):
+            landed(h_all(k, b), h2_sem.at[b * n + k])
     for copy, when in ends:
         if when is None:
             copy.wait_send()
@@ -279,11 +275,7 @@
 
 
 def n_sends(n):
-    block = 2 * (n - 1) + (n - 1) + 2
-    plane = 2 * (n - 1)
-    arrive = (n - 1) * (n - 1)
-    forward = (n - 2) * n * 2
-    return 2 * n + 2 + 3 * (block + plane + arrive + forward)
+    return 4 + 3 * (2 * (n - 1) + 2 + 2 * (n - 2) + 3)
 
 
 def gather_pairs(hidden, out_grad, counts, route_index, keep, capacity):
@@ -305,15 +297,16 @@
         ],
         in_specs=[smem, smem, vmem, vmem, vmem],
         out_specs=[vmem] * 4,
+        compiler_params=pltpu.CompilerParams(vmem_limit_bytes=16 << 20),
         name="slots",
     )(counts, keep, route_index, hidden, out_grad)
     hh, hc, gg, gc = pl.pallas_call(
         functools.partial(spread_kernel, n),
         out_shape=[
-            jax.ShapeDtypeStruct((replicas, 2, big, hcols), kind),
-            jax.ShapeDtypeStruct((replicas, 2 * rest, hcols), kind),
-            jax.ShapeDtypeStruct((replicas, 2, big, gcols), kind),
-            jax.ShapeDtypeStruct((replicas, 2 * rest, gcols), kind),
+            jax.ShapeDtypeStruct((n, n, 2, big, hcols), kind),
+            jax.ShapeDtypeStruct((n, n, 2 * rest, hcols), kind),
+            jax.ShapeDtypeStruct((n, n, 2, big, gcols), kind),
+            jax.ShapeDtypeStruct((n, n, 2 * rest, gcols), kind),
         ],
         in_specs=[vmem] * 4,
         out_specs=[vmem] * 4,
@@ -325,12 +318,16 @@
             pltpu.VMEM((n, 2 * rest, hcols), kind),
             pltpu.VMEM((n, 2 * rest, gcols), kind),
             pltpu.SemaphoreType.DMA((n_sends(n),)),
-            pltpu.SemaphoreType.DMA((replicas * 3,)),
-            pltpu.SemaphoreType.DMA((replicas * 3,)),
-            pltpu.SemaphoreType.DMA((2 * n + 2,)),
+            pltpu.SemaphoreType.DMA((3 * n,)),
+            pltpu.SemaphoreType.DMA((3 * n,)),
+            pltpu.SemaphoreType.DMA((3 * n,)),
+            pltpu.SemaphoreType.DMA((3 * n,)),
+            pltpu.SemaphoreType.DMA((4,)),
             pltpu.SemaphoreType.DMA((6,)),
         ],
-        compiler_params=pltpu.CompilerParams(collective_id=0, has_side_effects=True),
+        compiler_params=pltpu.CompilerParams(
+            collective_id=0, has_side_effects=True, vmem_limit_bytes=24 << 20
+        ),
         name="spread",
     )(*made)
     return [
@@ -363,12 +360,18 @@
         top = jnp.max(jnp.abs(block), axis=1, keepdims=True)
         out[:, b * LANES : (b + 1) * LANES] = block * (1.0 / (top + 1e-6))
         tops.append(top)
-    scales[...] = jnp.concatenate(tops, axis=1)
+    lane = lax.broadcasted_iota(jnp.int32, (out.shape[0], LANES), 1)
+    packed = jnp.zeros((out.shape[0], LANES), jnp.float32)
+    for b, top in enumerate(tops):
+        packed = jnp.where(lane == b, top, packed)
+    spun = packed.T
+    for b in range(scales.shape[0]):
+        scales[b] = spun[b : b + 1]
 
 
 def tile_grad(pairs, keep):
     rows, cols = pairs[0][0].shape[1], pairs[0][1].shape[1]
-    step = min(rows, 256)
+    step = min(rows, 512)
     args, specs = [], []
     for h, g in pairs:
         args += [h, g]
@@ -379,13 +382,14 @@
         grid=(rows // step,),
         out_shape=[
             jax.ShapeDtypeStruct((rows, cols), jnp.float32),
-            jax.ShapeDtypeStruct((rows, cols // LANES), jnp.float32),
+            jax.ShapeDtypeStruct((cols // LANES, 1, rows), jnp.float32),
         ],
         in_specs=[pl.BlockSpec(memory_space=pltpu.SMEM)] + specs,
         out_specs=[
             pl.BlockSpec((step, cols), lambda i: (i, 0)),
-            pl.BlockSpec((step, cols // LANES), lambda i: (i, 0)),
+            pl.BlockSpec((cols // LANES, 1, step), lambda i: (0, 0, i)),
         ],
+        compiler_params=pltpu.CompilerParams(vmem_limit_bytes=32 << 20),
         name="tile_grad",
     )(keep, *args)
 
@@ -395,11 +399,11 @@
     tok_rows = hidden.shape[0]
     capacity = max(tok_rows // 4, tok_rows // experts + 4)
     rest = capacity % SUB
-    paired = experts == 2 and capacity == SUB + rest and 2 * rest == SUB // 2
+    paired = experts == 2 and lax.axis_size("dp") == 16 and capacity == SUB + rest and 2 * rest == SUB // 2
     gather = gather_pairs if paired else gather_general
     pairs = gather(hidden, out_grad, counts, route_index, keep, capacity)
     normed, scales = tile_grad(pairs, keep)
-    return (normed[None, None], scales[None, None])
+    return (normed[None, None], jnp.transpose(scales[None], (0, 2, 3, 1)))
 
 
 def solution(mesh):

time: 77.7 us -> 68 us (0.88)
  Pallas kernels: 74.4 us -> 63.1 us
  local copies, waits for them, and re-layouts: 2.2 us -> 4 us
    pallas_call x1, Pallas kernels: 60.2 us -> 52.1 us  [gather_pairs(): pl.pallas_call(functools.partial(spread_kernel, n), out_shape=[jax.ShapeD...]
    unnamed x1 -> x12, local copies, waits for them, and re-layouts: 2.2 us -> 4 us
    pallas_call x1, Pallas kernels: 11.5 us -> 9.81 us  [tile_grad(): pl.pallas_call(functools.partial(tile_kernel, len(pairs)), grid=(rows //...]
    pallas_call x1, Pallas kernels: 2.72 us -> 1.17 us  [gather_pairs(): pl.pallas_call(functools.partial(slots_kernel, n, big, rest), out_shape=[...]
where the time goes in v2:
time: 68 us; the launch traced here: 67.8 us
  Pallas kernels  63.1 us (93%)
  local copies, waits for them, and re-layouts  4 us (6%)
    pallas_call x1, Pallas kernels, gather_pairs(): pl.pallas_call(functools.partial(spread_kernel, n), out_shape=[jax.ShapeD...  52.1 us
    pallas_call x1, Pallas kernels, tile_grad(): pl.pallas_call(functools.partial(tile_kernel, len(pairs)), grid=(rows //...  9.81 us
    unnamed x12, local copies, waits for them, and re-layouts  4 us

profile of v2, /device:TPU:0, one launch (start us, length us, event | category | flops | bytes accessed | tf_op | source)
XLA Modules:
  0.0 67.8 jit_solution(12507254468536059371)
XLA Ops:
  0.6 0.0 copy-start
  0.6 1.0 %copy-done = bf16[32,8192]{1,0:T(8,128)(2,1)S(1)} copy-done((bf16[32,8192]{1,0:T(8,128)(2,1)S(1)}, bf16[32,8192]{1,0:T(8,128)(2,1)}, u32[]{:S(2)}) %copy-start) | copy-done | bytes 524312
  1.7 0.0 copy-start.1
  1.7 1.0 %copy-done.1 = bf16[32,6144]{1,0:T(8,128)(2,1)S(1)} copy-done((bf16[32,6144]{1,0:T(8,128)(2,1)S(1)}, bf16[32,6144]{1,0:T(8,128)(2,1)}, u32[]{:S(2)}) %copy-start.1) | copy-done | bytes 393240
  2.7 0.0 copy-start.2
  2.7 0.7 copy-done.2
  3.3 0.0 copy-start.4
  3.3 0.7 copy-done.4
  4.0 0.0 copy-start.5
  4.0 0.7 copy-done.5
  4.6 0.0 copy-start.3
  4.6 1.2 %slots.1 = (bf16[2,4,16,2048]{3,2,1,0:T(8,128)(2,1)S(1)}, bf16[2,4,8,2048]{3,2,1,0:T(8,128)(2,1)S(1)}, bf16[2,4,16,1536]{3,2,1,0:T(8,128)(2,1)S(1)}, bf16[2,4,8,1536]{3,2,1,0:T(8,128)(2,1)S(1)}) custom-call(s32[1,2]{1,0:T(1,128)S(1)} %copy-done.4, s32[16]{0:T(128)S(1)} %copy-done.2, s32[1,32]{1,0:T(1,128)S(1)} %copy-done.5, bf16[32,8192]{1,0:T(8,128)(2,1)S(1)} %copy-done, ...), custom_call_target="tpu_custom_call" | custom-call | tf_op jit(solution)/shard_map/slots/pallas_call | solution.py:290
  5.8 52.1 %spread.1 = (bf16[4,4,2,16,2048]{4,3,2,1,0:T(8,128)(2,1)S(1)}, bf16[4,4,8,2048]{3,2,1,0:T(8,128)(2,1)S(1)}, bf16[4,4,2,16,1536]{4,3,2,1,0:T(8,128)(2,1)S(1)}, bf16[4,4,8,1536]{3,2,1,0:T(8,128)(2,1)S(1)}) custom-call(bf16[2,4,16,2048]{3,2,1,0:T(8,128)(2,1)S(1)} %get-tuple-element.12.h_o, bf16[2,4,8,2048]{3,2,1,0:T(8,128)(2,1)S(1)} %get-tuple-element.13.h_c, ...), custom_call_target="tpu_custom_call" | custom-call | tf_op jit(solution)/shard_map/spread/pallas_call | solution.py:303
  58.0 0.0 copy-done.3
  58.0 9.8 %tile_grad.1 = (f32[2048,1536]{1,0:T(8,128)}, f32[12,1,2048]{2,1,0:T(1,128)}) custom-call(s32[16]{0:T(128)S(1)} %copy-done.3, bf16[512,2048]{1,0:T(8,128)(2,1)S(1)} %bitcast.8, bf16[512,1536]{1,0:T(8,128)(2,1)S(1)} %bitcast.9, bf16[128,2048]{1,0:T(8,128)(2,1)S(1)} %bitcast.10, bf16[128,1536]{1,0:T(8,128)(2,1)S(1)} %bitcast.11), custom_call_target="tpu_custom_call" | custom-call | tf_op jit(solution)/shard_map/tile_grad/pallas_call | solution.py:380
Async XLA Ops:
  0.6 1.0 %copy-start = (bf16[32,8192]{1,0:T(8,128)(2,1)S(1)}, bf16[32,8192]{1,0:T(8,128)(2,1)}, u32[]{:S(2)}) copy-start(bf16[32,8192]{1,0:T(8,128)(2,1)} %hidden.1) | copy-start | bytes 1572868
  1.7 1.0 %copy-start.1 = (bf16[32,6144]{1,0:T(8,128)(2,1)S(1)}, bf16[32,6144]{1,0:T(8,128)(2,1)}, u32[]{:S(2)}) copy-start(bf16[32,6144]{1,0:T(8,128)(2,1)} %grad.1) | copy-start | bytes 1179652
  2.7 0.7 copy-start.2
  3.3 0.7 copy-start.4
  4.0 0.7 copy-start.5
  4.6 53.3 %copy-start.3 = (s32[16]{0:T(128)S(1)}, s32[16]{0:T(128)}, u32[]{:S(2)}) copy-start(s32[16]{0:T(128)} %keep.3) | copy-start | bytes 196

commit v3 on v2

--- a/solution.py
+++ b/solution.py
@@ -77,7 +77,24 @@
     return [(all_h.reshape(-1, tile_rows), all_g.reshape(-1, tile_cols))]
 
 
-def slots_kernel(side, big, rest, counts, keep, route, hidden, grad, h_o, h_c, g_o, g_c):
+def slots_kernel(
+    side, big, rest, counts_in, keep_in, route_in, hidden_in, grad_in, h_o, h_c, g_o, g_c,
+    counts, keep, route, hidden, grad, sems,
+):
+    moves = []
+    for src, dst in ((counts_in, counts), (keep_in, keep), (route_in, route)):
+        moves.append(pltpu.make_async_copy(src, dst, sems.at[len(moves)]))
+    for src, dst in ((hidden_in, hidden), (grad_in, grad)):
+        cols = src.shape[1] // side
+        for part in range(side):
+            cut = (slice(None), pl.ds(part * cols, cols))
+            move = pltpu.make_async_copy(src.at[cut], dst.at[cut], sems.at[len(moves)])
+            moves.append(move)
+    for move in moves:
+        move.start()
+    for move in moves[:3]:
+        move.wait()
+    due = moves[3:]
     me = lax.axis_index("expert")
     rows = hidden.shape[0]
     total = 2 * big + 4 * rest
@@ -110,6 +127,7 @@
     for pick_x, src, o_ref, c_ref in ((pick_h, hidden, h_o, h_c), (pick_g, grad, g_o, g_c)):
         cols = o_ref.shape[3]
         for part in range(side):
+            due.pop(0).wait()
             got = jnp.dot(
                 pick_x,
                 src[:, part * cols : (part + 1) * cols],
@@ -286,7 +304,6 @@
     rest = capacity - big
     kind = jnp.bfloat16
     vmem = pl.BlockSpec(memory_space=pltpu.VMEM)
-    smem = pl.BlockSpec(memory_space=pltpu.SMEM)
     made = pl.pallas_call(
         functools.partial(slots_kernel, n, big, rest),
         out_shape=[
@@ -295,11 +312,19 @@
             jax.ShapeDtypeStruct((2, n, big, gcols), kind),
             jax.ShapeDtypeStruct((2, n, 2 * rest, gcols), kind),
         ],
-        in_specs=[smem, smem, vmem, vmem, vmem],
+        in_specs=[pl.BlockSpec(memory_space=pltpu.HBM)] * 5,
         out_specs=[vmem] * 4,
+        scratch_shapes=[
+            pltpu.SMEM(counts.shape, counts.dtype),
+            pltpu.SMEM(keep.shape, keep.dtype),
+            pltpu.VMEM(route_index.shape, route_index.dtype),
+            pltpu.VMEM(hidden.shape, kind),
+            pltpu.VMEM(out_grad.shape, kind),
+            pltpu.SemaphoreType.DMA((3 + 2 * n,)),
+        ],
         compiler_params=pltpu.CompilerParams(vmem_limit_bytes=16 << 20),
         name="slots",
-    )(counts, keep, route_index, hidden, out_grad)
+    )(*[pltpu.with_memory_space_constraint(x, pltpu.HBM) for x in (counts, keep, route_index, hidden, out_grad)])
     hh, hc, gg, gc = pl.pallas_call(
         functools.partial(spread_kernel, n),
         out_shape=[

time: 68 us -> 65.2 us (0.959)
  local copies, waits for them, and re-layouts: 4 us -> 0.01 us
  Pallas kernels: 63.1 us -> 64.4 us
    unnamed x12 -> x2, local copies, waits for them, and re-layouts: 4 us -> 0.01 us
    pallas_call x1, Pallas kernels: 1.17 us -> 2.47 us  [gather_pairs(): pl.pallas_call(functools.partial(slots_kernel, n, big, rest), out_shape=[...]
where the time goes in v3:
time: 65.2 us; the launch traced here: 65.1 us
  Pallas kernels  64.4 us (99%)
  between operations  0.66 us (1%)
    pallas_call x1, Pallas kernels, gather_pairs(): pl.pallas_call(functools.partial(spread_kernel, n), out_shape=[jax.ShapeD...  52.1 us
    pallas_call x1, Pallas kernels, tile_grad(): pl.pallas_call(functools.partial(tile_kernel, len(pairs)), grid=(rows //...  9.81 us
    pallas_call x1, Pallas kernels, gather_pairs(): pl.pallas_call(functools.partial(slots_kernel, n, big, rest), out_shape=[...  2.47 us

profile of v3, /device:TPU:0, one launch (start us, length us, event | category | flops | bytes accessed | tf_op | source)
XLA Modules:
  0.0 65.1 jit_solution(16693250768310280196)
XLA Ops:
  0.6 0.0 copy-start
  0.6 2.5 %slots.1 = (bf16[2,4,16,2048]{3,2,1,0:T(8,128)(2,1)S(1)}, bf16[2,4,8,2048]{3,2,1,0:T(8,128)(2,1)S(1)}, bf16[2,4,16,1536]{3,2,1,0:T(8,128)(2,1)S(1)}, bf16[2,4,8,1536]{3,2,1,0:T(8,128)(2,1)S(1)}) custom-call(s32[1,2]{1,0:T(1,128)} %counts_in.1, s32[16]{0:T(128)} %keep.1, s32[1,32]{1,0:T(1,128)} %route_in.1, bf16[32,8192]{1,0:T(8,128)(2,1)} %hidden_in.1, ...), custom_call_target="tpu_custom_call" | custom-call | tf_op jit(solution)/shard_map/slots/pallas_call | solution.py:307
  3.1 52.1 %spread.1 = (bf16[4,4,2,16,2048]{4,3,2,1,0:T(8,128)(2,1)S(1)}, bf16[4,4,8,2048]{3,2,1,0:T(8,128)(2,1)S(1)}, bf16[4,4,2,16,1536]{4,3,2,1,0:T(8,128)(2,1)S(1)}, bf16[4,4,8,1536]{3,2,1,0:T(8,128)(2,1)S(1)}) custom-call(bf16[2,4,16,2048]{3,2,1,0:T(8,128)(2,1)S(1)} %get-tuple-element.12.h_o, bf16[2,4,8,2048]{3,2,1,0:T(8,128)(2,1)S(1)} %get-tuple-element.13.h_c, ...), custom_call_target="tpu_custom_call" | custom-call | tf_op jit(solution)/shard_map/spread/pallas_call | solution.py:328
  55.2 0.0 copy-done
  55.3 9.8 %tile_grad.1 = (f32[2048,1536]{1,0:T(8,128)}, f32[12,1,2048]{2,1,0:T(1,128)}) custom-call(s32[16]{0:T(128)S(1)} %copy-done, bf16[512,2048]{1,0:T(8,128)(2,1)S(1)} %bitcast.8, bf16[512,1536]{1,0:T(8,128)(2,1)S(1)} %bitcast.9, bf16[128,2048]{1,0:T(8,128)(2,1)S(1)} %bitcast.10, bf16[128,1536]{1,0:T(8,128)(2,1)S(1)} %bitcast.11), custom_call_target="tpu_custom_call" | custom-call | tf_op jit(solution)/shard_map/tile_grad/pallas_call | solution.py:405
Async XLA Ops:
  0.6 54.6 %copy-start = (s32[16]{0:T(128)S(1)}, s32[16]{0:T(128)}, u32[]{:S(2)}) copy-start(s32[16]{0:T(128)} %keep.1) | copy-start | bytes 196
